TPU v7x, 32 devices: a whole 2x2x4 slice. The times are simulated.
32 devices in a mesh: tm: 16 (over z, y, x), space: 2 (over core).
Axes of the slice: x: 2, y: 2, z: 4, core: 2. Of those that a mesh axis runs over, the one named last changes fastest.
Arguments:
- snapshots: bfloat16 [8192, 16384], P('tm', 'space'), may hold values from -40 to 40
- exponents: float32 [2, 32], replicated, may hold values from -150 to 150, as said below
Outputs:
- new_exponents: float32 [2, 32], replicated
- amplitudes: float32 [2, 32, 16384], P(None, None, 'space')
- residual: bfloat16 [8192, 16384], P('tm', 'space')
Inputs may be any that keep to these rules, and one draw needn't show every extreme that they name: `exponents`: row 0 lies in -2.3 to 0.8, row 1 in -150 to 150.
All inputs are finite; a program needn't handle non-finite values.
Results may differ from a plain program's by a relative error of at most 0.0012.
The roundings to bfloat16 on the way count: a program that leaves them out, or rounds other values in their place, can miss the bound.
Values sent between devices are 32-bit elements; how exact they have to be, the bound alone decides.
A program may use at most 64 MiB of HBM per device.

v0:
```python
import jax
import jax.numpy as jnp
from jax import lax
from jax.sharding import PartitionSpec as P

damping = 0.01


def factor_solve(factor, right):
    lower_part = lax.linalg.triangular_solve(factor, right, left_side=True, lower=True)
    return lax.linalg.triangular_solve(
        factor, lower_part, left_side=True, lower=True, transpose_a=True
    )


def make_basis(exponents, time_grid):
    magnitude = jnp.exp(time_grid[:, None] * exponents[0][None, :])
    phase_angle = time_grid[:, None] * exponents[1][None, :]
    plain = jnp.concatenate([magnitude * jnp.cos(phase_angle), magnitude * jnp.sin(phase_angle)], 1)
    return jnp.concatenate([plain, time_grid[:, None] * plain], 1)


def inner_product(left, right):
    return lax.dot_general(
        left,
        right,
        (((0,), (0,)), ((), ())),
        precision=lax.Precision.HIGHEST,
        preferred_element_type=jnp.float32,
    )


def hermitian(blocks, modes):
    return (
        blocks[:modes, :modes] + blocks[modes:, modes:],
        blocks[:modes, modes:] - blocks[modes:, :modes],
    )


def embedded(real_part, imag_part):
    return jnp.concatenate(
        [jnp.concatenate([real_part, -imag_part], 1), jnp.concatenate([imag_part, real_part], 1)], 0
    )


def sign_flip(modes):
    return jnp.concatenate([jnp.ones((modes,), jnp.float32), -jnp.ones((modes,), jnp.float32)])


def basis_solve(gram_matrix, modes):
    double = 2 * modes
    g_real, g_imag = hermitian(gram_matrix[:double, :double], modes)
    factor = jnp.linalg.cholesky(embedded(g_real, g_imag))
    return factor_solve(factor, jnp.eye(double, dtype=jnp.float32))


def amplitude_rows(inverse_g, projections, modes):
    left_solve = inverse_g * sign_flip(modes)[None, :]
    return lax.dot_general(
        left_solve,
        projections[:, : 2 * modes],
        (((1,), (1,)), ((), ())),
        precision=lax.Precision.HIGHEST,
        preferred_element_type=jnp.float32,
    )


def self_only(amp_rows):
    return lax.dot_general(
        amp_rows,
        amp_rows,
        (((1,), (1,)), ((), ())),
        precision=lax.Precision.HIGHEST,
        preferred_element_type=jnp.float32,
    )


def fit_terms(amp_rows, projections, modes):
    double = 2 * modes
    self_terms = self_only(amp_rows)
    cross = (
        jnp.dot(
            amp_rows,
            projections[:, double:],
            precision=lax.Precision.HIGHEST,
            preferred_element_type=jnp.float32,
        )
        * sign_flip(modes)[None, :]
    )
    v_real = jnp.diagonal(cross[:modes, :modes]) + jnp.diagonal(cross[modes:, modes:])
    v_imag = jnp.diagonal(cross[:modes, modes:]) - jnp.diagonal(cross[modes:, :modes])
    return (self_terms, jnp.stack([v_real, v_imag]))


def lm_update(exponents, gram_matrix, inverse_g, self_terms, cross_sums, modes):
    double = 2 * modes
    c_real, c_imag = hermitian(gram_matrix[:double, double:], modes)
    e_real, e_imag = hermitian(gram_matrix[double:, double:], modes)
    coupling = embedded(c_real, c_imag)
    through = jnp.dot(coupling.T, inverse_g, precision=lax.Precision.HIGHEST)
    reduced = embedded(e_real, e_imag) - jnp.dot(through, coupling, precision=lax.Precision.HIGHEST)
    m_real = reduced[:modes, :modes]
    m_imag = reduced[modes:, :modes]
    s_real, s_imag = hermitian(self_terms, modes)
    w_real = jnp.sum(c_real.T * s_real + c_imag.T * s_imag, 1)
    w_imag = jnp.sum(c_real.T * s_imag - c_imag.T * s_real, 1)
    grad_real = w_real - cross_sums[0]
    grad_imag = w_imag - cross_sums[1]
    h_real = s_real * m_real - s_imag * m_imag + damping * jnp.eye(modes, dtype=jnp.float32)
    h_imag = s_real * m_imag + s_imag * m_real
    factor = jnp.linalg.cholesky(embedded(h_real, h_imag))
    step_vector = factor_solve(factor, jnp.concatenate([grad_real, grad_imag])[:, None])[:, 0]
    return exponents - jnp.stack([step_vector[:modes], step_vector[modes:]])


def shards(snapshots, exponents):
    local_rows = snapshots.shape[0]
    columns = snapshots.shape[1]
    modes = exponents.shape[1]
    groups = lax.axis_size("tm")
    all_rows = local_rows * groups
    first_row = lax.axis_index("tm") * local_rows
    grid_all = jnp.arange(all_rows, dtype=jnp.int32).astype(jnp.float32) / all_rows
    basis_all = make_basis(exponents, grid_all)
    gram_matrix = inner_product(basis_all, basis_all)
    basis = lax.dynamic_slice_in_dim(basis_all, first_row, local_rows, 0)
    basis_b = basis.astype(jnp.bfloat16)
    inverse_g = basis_solve(gram_matrix, modes)
    local_proj = lax.dot_general(
        snapshots, basis_b, (((0,), (0,)), ((), ())), preferred_element_type=jnp.float32
    )
    projections = lax.psum(local_proj, "tm")
    amp_rows = amplitude_rows(inverse_g, projections, modes)
    self_terms, cross_sums = fit_terms(amp_rows, projections, modes)
    self_terms, cross_sums = lax.psum((self_terms, cross_sums), "space")
    new_exponents = lm_update(exponents, gram_matrix, inverse_g, self_terms, cross_sums, modes)
    signed = (amp_rows * sign_flip(modes)[:, None]).astype(jnp.bfloat16)
    fitted = jnp.dot(basis_b[:, : 2 * modes], signed, preferred_element_type=jnp.float32)
    residual = (snapshots.astype(jnp.float32) - fitted).astype(jnp.bfloat16)
    return (new_exponents, amp_rows.reshape(2, modes, columns), residual)


def solution(mesh):
    return jax.shard_map(
        shards,
        mesh=mesh,
        in_specs=(P("tm", "space"), P()),
        out_specs=(P(), P(None, None, "space"), P("tm", "space")),
        check_vma=False,
    )
```

profile of v0, /device:TPU:0, one launch (start us, length us, event | category | flops | bytes accessed | tf_op | source)
XLA Modules:
  0.0 238.0 jit_solution(3931812561090140214)
XLA Ops:
  7.2 0.8 slice_bitcast_fusion.3
  8.0 3.9 %fusion.7 = (f32[8192,32]{0,1:T(8,128)S(1)}, f32[8192,32]{0,1:T(8,128)S(1)}) fusion(f32[32]{0:T(128)S(1)} %get-tuple-element.36, f32[32]{0:T(128)S(1)} %get-tuple-element.35, f32[8192]{0:T(1024)S(1)} %convert_multiply_fusion), kind=kLoop, calls=%fused_computation.19 | loop fusion | flops 1048576 | bytes 2130176 | tf_op jit(solution)/shard_map/mul | solution.py:19
  11.9 0.1 maximum_multiply_fusion
  12.0 1.3 copy-done.1
  13.3 1.6 pad_maximum_fusion
  15.0 0.9 dynamic-slice_convert_fusion
  15.9 6.7 %convolution_bitcast_fusion = f32[8192,128]{0,1:T(8,128)} fusion(bf16[512,128]{0,1:T(8,128)(2,1)S(1)} %dynamic-slice_convert_fusion, bf16[512,8192]{1,0:T(8,128)(2,1)} %param.3), kind=kOutput, calls=%fused_computation.5 | convolution fusion | flops 1073741824 | bytes 12713984 | tf_op jit(solution)/shard_map/dot_general | solution.py:129
  22.6 5.6 %fusion.35 = f32[128,128]{1,0:T(8,128)S(1)} fusion(f32[8192,64]{0,1:T(8,128)} %copy-done.1, f32[8192,32]{0,1:T(8,128)S(1)} %get-tuple-element.28, f32[8192,32]{0,1:T(8,128)S(1)} %get-tuple-element.27), kind=kOutput, calls=%fused_computation.85 | convolution fusion | flops 1612709888 | bytes 4259840 | tf_op jit(solution)/shard_map/dot_general | solution.py:24
  28.2 0.1 fusion.39
  28.3 0.1 copy.50
  28.5 0.1 copy.45
  28.6 0.1 copy.43
  28.8 0.1 copy.49
  28.9 0.1 maximum_maximum_fusion
  29.0 0.1 copy.33
  29.1 0.1 fusion.20
  29.2 5.9 %cholesky.44 = f32[64,64]{1,0:T(8,128)S(1)} custom-call(f32[64,64]{1,0:T(8,128)S(1)} %fusion.20), custom_call_target="Cholesky" | custom-call | tf_op jit(solution)/shard_map/jit(cholesky)/cholesky | solution.py:53
  35.1 0.6 compare_reduce_fusion.1
  35.7 0.7 fusion.11
  36.4 4.9 %custom-call.12 = f32[1,64,64]{1,2,0:T(8,128)S(1)} custom-call(f32[1,64,64]{2,1,0:T(8,128)S(1)} %fusion.11), custom_call_target="InvertDiagBlocksLowerTriangular" | custom-call | tf_op jit(solution)/shard_map/triangular_solve | solution.py:11
  41.3 0.2 fusion.18
  41.5 0.2 fusion.16
  41.7 152.1 %all-reduce.3.cloned.1.call-done = f32[8192,128]{0,1:T(8,128)} async-done(((f32[8192,128]{0,1:T(8,128)}), f32[8192,128]{0,1:T(8,128)}) %all-reduce.3.cloned.1.call-update) | async-done | bytes 4194320 | tf_op jit(solution)/shard_map/psum | solution.py:132
  193.8 3.7 %fusion.2 = f32[64,8192]{1,0:T(8,128)S(1)} fusion(f32[8192,128]{0,1:T(8,128)} %all-reduce.3.cloned.1.call-done, f32[64,64]{1,0:T(8,128)S(1)} %fusion.16, f32[64]{0:T(128)S(1)} %copy-done.3), kind=kOutput, calls=%fused_computation.9 | convolution fusion | flops 402657280 | bytes 4210944 | tf_op jit(solution)/shard_map/dot_general | solution.py:59
  197.5 1.8 fusion.41
  199.3 9.4 %subtract_convert_fusion = bf16[512,8192]{1,0:T(8,128)(2,1)} fusion(bf16[512,8192]{1,0:T(8,128)(2,1)} %param.3, f32[64,8192]{1,0:T(8,128)S(1)} %fusion.2, f32[64]{0:T(128)S(1)} %copy-done.3, bf16[512,128]{0,1:T(8,128)(2,1)S(1)} %dynamic-slice_convert_fusion), kind=kOutput, calls=%fused_computation.4 | convolution fusion | flops 550502400 | bytes 18940416 | tf_op jit(solution)/shard_map/dot_general | solution.py:138
  208.7 1.8 fusion.4
  210.5 0.1 fusion.40
  210.6 0.7 gather_fusion.1
  211.3 0.7 gather_fusion.3
  212.0 0.7 gather_fusion.2
  212.7 0.7 gather_fusion
  213.5 3.5 %all-reduce = (f32[64,64]{0,1:T(8,128)S(1)}, f32[2,32]{1,0:T(2,128)S(1)}) all-reduce(f32[64,64]{0,1:T(8,128)S(1)} %fusion.41, f32[2,32]{1,0:T(2,128)S(1)} %pad_maximum_fusion.1), channel_id=1, replica_groups=mesh['tm'=16,'space'=2] {'space'}, use_global_device_ids=true, to_apply=%region_3.5 | all-reduce | flops 4160 | bytes 33280 | tf_op jit(solution)/shard_map/psum | solution.py:135
  216.9 0.1 fusion.25
  217.1 0.3 fusion.29
  217.4 0.3 convolution_subtract_fusion
  217.7 0.1 fusion.36
  217.8 0.1 maximum_maximum_fusion.2
  217.8 0.1 copy.40
  217.9 0.1 fusion.15
  218.0 5.9 %cholesky.55 = f32[64,64]{1,0:T(8,128)S(1)} custom-call(f32[64,64]{1,0:T(8,128)S(1)} %fusion.15), custom_call_target="Cholesky" | custom-call | tf_op jit(solution)/shard_map/jit(cholesky)/cholesky | solution.py:111
  223.9 0.6 compare_reduce_fusion
  224.5 0.7 fusion.12
  225.2 4.9 %custom-call.13 = f32[1,64,64]{1,2,0:T(8,128)S(1)} custom-call(f32[1,64,64]{2,1,0:T(8,128)S(1)} %fusion.12), custom_call_target="InvertDiagBlocksLowerTriangular" | custom-call | tf_op jit(solution)/shard_map/triangular_solve | solution.py:11
  230.1 0.2 convolution_bitcast_fusion.2
  230.3 0.2 convolution_bitcast_fusion.1
  230.5 0.1 slice_bitcast_fusion.1
  230.6 0.6 maximum_subtract_fusion
  (27 shorter events, 0.5 us)
Async XLA Ops:
  7.2 186.6 %all-reduce.3.cloned.1.call-start = ((), (), s32[]{:S(2)}) async-start(), calls=%async_computation | async-start | bytes 8388608 | tf_op jit(solution)/shard_map/psum | solution.py:132
  12.0 1.3 copy-start.1
  22.6 171.2 %copy-start.3 = (f32[64]{0:T(128)S(1)}, f32[64]{0:T(128)}, u32[]{:S(2)}) copy-start(f32[64]{0:T(128)} %constant.71.clone.1) | copy-start | bytes 772
  197.5 11.2 %copy-start = (f32[64,8192]{1,0:T(8,128)}, f32[64,8192]{1,0:T(8,128)S(1)}, u32[]{:S(2)}) copy-start(f32[64,8192]{1,0:T(8,128)S(1)} %fusion.2) | copy-start | bytes 6291460
  199.3 9.4 %copy-start.2 = (f32[8192,128]{0,1:T(8,128)S(1)}, f32[8192,128]{0,1:T(8,128)}, u32[]{:S(2)}) copy-start(f32[8192,128]{0,1:T(8,128)} %all-reduce.3.cloned.1.call-done) | copy-start | bytes 12582916
  210.5 20.1 %copy-start.4 = (f32[2,32]{1,0:T(2,128)S(1)}, f32[2,32]{1,0:T(2,128)}, u32[]{:S(2)}) copy-start(f32[2,32]{1,0:T(2,128)} %param.4) | copy-start | bytes 772
Sparse Core Ops, SparseCore 0:
  22.7 171.0 all-reduce.2
where the time goes:
time: 238 us
  waiting for transfers between devices  152 us (64%)
  other arithmetic  31 us (13%)
  matrix products  30.3 us (13%)
  between operations  14.3 us (6%)
  local copies, waits for them, and re-layouts  6.82 us (3%)
  blocking collectives  3.45 us (1%)
    psum x1, waiting for transfers between devices, shards(): projections = lax.psum(local_proj, 'tm')  152 us
    another operation x4, other arithmetic, factor_solve(): lax.linalg.triangular_solve(factor, lower_part, left_side=True, lower=Tru...  11.1 us
    dot_general x1, matrix products, shards(): jnp.dot(basis_b[:, :2 * modes], signed, preferred_element_type=jnp.float32)  9.35 us
    dot_general x1, matrix products, shards(): lax.dot_general(snapshots, basis_b, (((0,), (0,)), ((), ())), preferred_e...  6.66 us
    another operation x3, other arithmetic, basis_solve(): factor = jnp.linalg.cholesky(embedded(g_real, g_imag))  6.53 us
    another operation x3, other arithmetic, lm_update(): factor = jnp.linalg.cholesky(embedded(h_real, h_imag))  6.53 us
    dot_general x1, matrix products, inner_product(): lax.dot_general(left, right, (((0,), (0,)), ((), ())), precision=lax.Prec...  5.63 us
  transfers between devices with their start and end apart: 1, of which 1 were waited for; matrix products, arithmetic and copies ran while one was open for 8% of the time, Pallas kernels for 0%

commit v1 on v0

v1 whole, which is shorter than its diff:
```python
import functools

import jax
import jax.numpy as jnp
from jax import lax
from jax.experimental import pallas as pl
from jax.experimental.pallas import tpu as pltpu
from jax.sharding import PartitionSpec as P

damping = 0.01
MESH = pl.DeviceIdType.MESH
LANES = 128
ORDERS = ((0, 1, 2), (1, 0, 2), (2, 0, 1), (1, 2, 0))


def exact_dot(left, right, dims=((1,), (0,))):
    return lax.dot_general(
        left,
        right,
        (dims, ((), ())),
        precision=lax.Precision.HIGHEST,
        preferred_element_type=jnp.float32,
    )


def complex_inverse(real, imag):
    modes = real.shape[0]
    rows = lax.broadcasted_iota(jnp.int32, real.shape, 0)
    cols = lax.broadcasted_iota(jnp.int32, real.shape, 1)
    for k in range(modes):
        on_row, on_col = rows == k, cols == k
        scale = 1.0 / real[k : k + 1, k : k + 1]
        row_r = jnp.where(on_col[:1], 1.0, real[k : k + 1, :]) * scale
        row_i = jnp.where(on_col[:1], 0.0, imag[k : k + 1, :]) * scale
        col_r, col_i = real[:, k : k + 1], imag[:, k : k + 1]
        real = jnp.where(
            on_row, row_r, jnp.where(on_col, 0.0, real) - (col_r * row_r - col_i * row_i)
        )
        imag = jnp.where(
            on_row, row_i, jnp.where(on_col, 0.0, imag) - (col_r * row_i + col_i * row_r)
        )
    return real, imag


def complex_dot(ar, ai, br, bi):
    return exact_dot(ar, br) - exact_dot(ai, bi), exact_dot(ar, bi) + exact_dot(ai, br)


def exchange_kernel(
    modes, tm_bits, sp_bits, parts,
    yz_ref, gram_ref, exps_ref,
    amp_ref, new_ref,
    full, halves, gsum, grecv, ssum, srecv, vsum, vrecv,
    rs_send, rs_recv, ag_send, ag_recv,
    g_send, g_recv, s_send, s_recv, v_send, v_recv, out_sem,
):
    double = 2 * modes
    columns = full.shape[1]
    width = columns // parts
    me, sp = lax.axis_index("tm"), lax.axis_index("space")
    swap = sp % 2

    def stride_of(bit):
        if tm_bits >= 2 and bit == 0:
            return 1 + swap
        if tm_bits >= 2 and bit == 1:
            return 2 - swap
        return 2**bit

    def flip(index, stride):
        side = (index // stride) % 2
        return side, index + (1 - 2 * side) * stride

    friends = [(flip(me, 2**b)[1], sp) for b in range(tm_bits)]
    friends += [(me, flip(sp, 2**b)[1]) for b in range(sp_bits)]

    barrier = pltpu.get_barrier_semaphore()
    for friend in friends:
        pl.semaphore_signal(barrier, inc=1, device_id=friend, device_id_type=MESH)
    pl.semaphore_wait(barrier, len(friends))

    def remote(src, dst, send, recv, friend):
        copy = pltpu.make_async_remote_copy(
            src_ref=src, dst_ref=dst, send_sem=send, recv_sem=recv,
            device_id=friend, device_id_type=MESH,
        )
        copy.start()
        return copy

    sends = []

    def sum_start(stage, total, landed, send, recv):
        copy = remote(
            total.at[stage], landed.at[stage], send.at[stage], recv.at[stage], friends[stage]
        )
        sends.append(copy)
        return copy

    def sum_end(stage, copy, total, landed):
        copy.wait_recv()
        total[stage + 1] = total[stage] + landed[stage]

    plan = []
    for p in range(parts):
        first = [b for b in ORDERS[p % len(ORDERS)] if b < tm_bits]
        order = first + [b for b in range(tm_bits) if b not in first]
        plan.append([flip(me, stride_of(b)) for b in order])

    def lanes(start, size):
        return pl.ds(pl.multiple_of(start, LANES), size)

    def scatter_start(p, s):
        side, partner = plan[p][s]
        size = width >> (s + 1)
        away = (1 - side) * size
        if s == 0:
            src = yz_ref.at[pl.ds(0, double), lanes(p * width + away, size)]
        else:
            src = halves[s - 1].at[p, :, lanes(away, size)]
        copy = remote(src, halves[s].at[p], rs_send.at[p, s], rs_recv.at[p, s], (partner, sp))
        sends.append(copy)
        return copy

    def scatter_add(p, s):
        side, _ = plan[p][s]
        size = width >> (s + 1)
        keep = side * size
        if s == 0:
            mine = yz_ref[pl.ds(0, double), lanes(p * width + keep, size)]
        else:
            mine = halves[s - 1][p, :, lanes(keep, size)]
        halves[s][p] = halves[s][p] + mine

    gsum[0] = gram_ref[...]
    flying = [scatter_start(p, 0) for p in range(parts)]
    g_copy = sum_start(0, gsum, grecv, g_send, g_recv)
    for s in range(tm_bits):
        sum_end(s, g_copy, gsum, grecv)
        if s + 1 < tm_bits:
            g_copy = sum_start(s + 1, gsum, grecv, g_send, g_recv)
            for p in range(parts):
                flying[p].wait_recv()
                scatter_add(p, s)
                flying[p] = scatter_start(p, s + 1)

    blocks = gsum[tm_bits]

    def block(index):
        moved = blocks if index == 0 else pltpu.roll(blocks, LANES - index * modes, 1)
        return moved[:modes, :modes], moved[modes:, :modes]

    g_r, g_i = block(0)
    c_r, c_i = block(1)
    e_r, e_i = block(2)
    inv_r, inv_i = complex_inverse(g_r, g_i)
    t_r, t_i = complex_dot(inv_r, inv_i, c_r, c_i)
    u_r, u_i = complex_dot(c_r, c_i, t_r, t_i)
    m_r, m_i = e_r - u_r, e_i - u_i

    offsets = []
    self_r = jnp.zeros((modes, modes), jnp.float32)
    self_i = jnp.zeros((modes, modes), jnp.float32)
    last = tm_bits - 1

    def gather_start(p, s):
        size = width >> (s + 1)
        where = full.at[:, lanes(offsets[p], size)]
        _, partner = plan[p][s]
        copy = remote(where, where, ag_send.at[p, s], ag_recv.at[p, s], (partner, sp))
        sends.append(copy)
        return copy

    for p in range(parts):
        flying[p].wait_recv()
        scatter_add(p, last)
        own = halves[last][p]
        a_r, a_i = complex_dot(inv_r, inv_i, own[:modes], own[modes:])
        start = p * width
        for s in range(tm_bits):
            start = start + plan[p][s][0] * (width >> (s + 1))
        offsets.append(start)
        size = width >> tm_bits
        full[pl.ds(0, modes), lanes(start, size)] = a_r
        full[pl.ds(modes, modes), lanes(start, size)] = a_i
        flying[p] = gather_start(p, last)
        over = ((1,), (1,))
        self_r += exact_dot(a_r, a_r, over) + exact_dot(a_i, a_i, over)
        self_i += exact_dot(a_r, a_i, over) - exact_dot(a_i, a_r, over)

    ssum[0] = jnp.zeros(ssum.shape[1:], jnp.float32)
    ssum[0, pl.ds(0, modes), pl.ds(0, modes)] = self_r
    ssum[0, pl.ds(modes, modes), pl.ds(0, modes)] = self_i
    s_copy = sum_start(0, ssum, srecv, s_send, s_recv)
    s_stage = 0
    steps = len(friends)
    for s in range(last, 0, -1):
        sum_end(s_stage, s_copy, ssum, srecv)
        s_stage += 1
        s_copy = sum_start(s_stage, ssum, srecv, s_send, s_recv)
        for p in range(parts):
            flying[p].wait_recv()
            offsets[p] = offsets[p] - plan[p][s][0] * (width >> (s + 1))
            flying[p] = gather_start(p, s - 1)
    while s_stage < steps:
        sum_end(s_stage, s_copy, ssum, srecv)
        s_stage += 1
        if s_stage < steps:
            s_copy = sum_start(s_stage, ssum, srecv, s_send, s_recv)

    s_r = ssum[steps, pl.ds(0, modes), pl.ds(0, modes)]
    s_i = ssum[steps, pl.ds(modes, modes), pl.ds(0, modes)]
    square = (modes, modes)
    diagonal = lax.broadcasted_iota(jnp.int32, square, 0) == lax.broadcasted_iota(
        jnp.int32, square, 1
    )
    h_r = s_r * m_r - s_i * m_i + jnp.where(diagonal, damping, 0.0)
    h_i = s_r * m_i + s_i * m_r
    hinv_r, hinv_i = complex_inverse(h_r, h_i)
    w_r = jnp.sum(c_r * s_r - c_i * s_i, 1, keepdims=True)
    w_i = jnp.sum(c_r * s_i + c_i * s_r, 1, keepdims=True)

    v_r = jnp.zeros((modes, LANES), jnp.float32)
    v_i = jnp.zeros((modes, LANES), jnp.float32)
    outs = []
    for p in range(parts):
        flying[p].wait_recv()
        part = pl.ds(p * width, width)
        out = pltpu.make_async_copy(full.at[:, part], amp_ref.at[:, part], out_sem.at[p])
        out.start()
        outs.append(out)
        run = 4

        def step(i, carry, p=p):
            v_r, v_i = carry
            for j in range(run):
                at = lanes(p * width + (i * run + j) * LANES, LANES)
                a_r, a_i = full[pl.ds(0, modes), at], full[pl.ds(modes, modes), at]
                z_r = yz_ref[pl.ds(double, modes), at]
                z_i = yz_ref[pl.ds(double + modes, modes), at]
                v_r = v_r + (a_r * z_r + a_i * z_i)
                v_i = v_i + (a_r * z_i - a_i * z_r)
            return v_r, v_i

        v_r, v_i = lax.fori_loop(0, width // (run * LANES), step, (v_r, v_i))

    ones = jnp.ones((8, LANES), jnp.float32)
    vsum[0] = jnp.zeros(vsum.shape[1:], jnp.float32)
    vsum[0, pl.ds(0, 8), pl.ds(0, modes)] = exact_dot(ones, v_r, ((1,), (1,)))
    vsum[0, pl.ds(8, 8), pl.ds(0, modes)] = exact_dot(ones, v_i, ((1,), (1,)))
    for stage in range(steps):
        v_copy = sum_start(stage, vsum, vrecv, v_send, v_recv)
        sum_end(stage, v_copy, vsum, vrecv)

    def as_column(row):
        return jnp.sum(jnp.where(diagonal, row, 0.0), 1, keepdims=True)

    grad_r = w_r - as_column(vsum[steps, pl.ds(0, 1), pl.ds(0, modes)])
    grad_i = w_i - as_column(vsum[steps, pl.ds(8, 1), pl.ds(0, modes)])
    new_ref[pl.ds(0, 1), :] = exps_ref[pl.ds(0, 1), :] - jnp.sum(
        hinv_r * grad_r + hinv_i * grad_i, 0, keepdims=True
    )
    new_ref[pl.ds(1, 1), :] = exps_ref[pl.ds(1, 1), :] - jnp.sum(
        hinv_r * grad_i - hinv_i * grad_r, 0, keepdims=True
    )
    for out in outs:
        out.wait()
    for copy in sends:
        copy.wait_send()


def exchange(yz, gram, exponents, groups, spaces):
    modes = exponents.shape[1]
    double, columns = 2 * modes, yz.shape[1]
    tm_bits, sp_bits = groups.bit_length() - 1, spaces.bit_length() - 1
    assert groups == 2**tm_bits and spaces == 2**sp_bits
    parts = min(len(ORDERS), columns // (groups * LANES))
    steps = tm_bits + sp_bits
    width = columns // parts

    def buffer(*shape):
        return pltpu.VMEM(shape, jnp.float32)

    def dma(*shape):
        return pltpu.SemaphoreType.DMA(shape)

    vmem = pl.BlockSpec(memory_space=pltpu.VMEM)
    return pl.pallas_call(
        functools.partial(exchange_kernel, modes, tm_bits, sp_bits, parts),
        out_shape=(
            jax.ShapeDtypeStruct((double, columns), jnp.float32),
            jax.ShapeDtypeStruct(exponents.shape, jnp.float32),
        ),
        in_specs=[vmem] * 3,
        out_specs=(pl.BlockSpec(memory_space=pl.ANY), vmem),
        scratch_shapes=[
            buffer(double, columns),
            [buffer(parts, double, width >> (s + 1)) for s in range(tm_bits)],
            buffer(tm_bits + 1, double, LANES),
            buffer(tm_bits, double, LANES),
            buffer(steps + 1, double, LANES),
            buffer(steps, double, LANES),
            buffer(steps + 1, 16, LANES),
            buffer(steps, 16, LANES),
            dma(parts, tm_bits), dma(parts, tm_bits),
            dma(parts, tm_bits), dma(parts, tm_bits),
            dma(tm_bits), dma(tm_bits),
            dma(steps), dma(steps),
            dma(steps), dma(steps),
            dma(parts),
        ],
        compiler_params=pltpu.CompilerParams(
            collective_id=0, has_side_effects=True, vmem_limit_bytes=32 * 2**20
        ),
    )(yz, gram, exponents)


def shards(snapshots, exponents):
    local_rows, columns = snapshots.shape
    modes = exponents.shape[1]
    groups, spaces = lax.axis_size("tm"), lax.axis_size("space")
    rows = lax.axis_index("tm") * local_rows + jnp.arange(local_rows, dtype=jnp.int32)
    time = (rows.astype(jnp.float32) / (local_rows * groups))[:, None]
    magnitude = jnp.exp(time * exponents[0][None, :])
    phase_angle = time * exponents[1][None, :]
    real, imag = magnitude * jnp.cos(phase_angle), magnitude * jnp.sin(phase_angle)
    plain = jnp.concatenate([real, -imag], 1)
    basis_b = jnp.concatenate([plain, time * plain], 1).astype(jnp.bfloat16)
    yz = lax.dot_general(
        basis_b, snapshots, (((0,), (0,)), ((), ())), preferred_element_type=jnp.float32
    )
    both = jnp.concatenate([plain, jnp.concatenate([imag, real], 1)], 0)
    twice = jnp.concatenate([time, time], 0)
    first = both[:, :modes]
    gram_gc = exact_dot(both, jnp.concatenate([first, twice * first], 1), ((0,), (0,)))
    gram_e = exact_dot(twice * both, twice * first, ((0,), (0,)))
    gram = jnp.concatenate(
        [gram_gc, gram_e, jnp.zeros((2 * modes, LANES - 3 * modes), jnp.float32)], 1
    )
    amp_rows, new_exponents = exchange(yz, gram, exponents, groups, spaces)
    fitted = jnp.dot(
        basis_b[:, : 2 * modes],
        amp_rows.astype(jnp.bfloat16),
        preferred_element_type=jnp.float32,
    )
    residual = (snapshots.astype(jnp.float32) - fitted).astype(jnp.bfloat16)
    return (new_exponents, amp_rows.reshape(2, modes, columns), residual)


def solution(mesh):
    return jax.shard_map(
        shards,
        mesh=mesh,
        in_specs=(P("tm", "space"), P()),
        out_specs=(P(), P(None, None, "space"), P("tm", "space")),
        check_vma=False,
    )
```

time: 238 us -> 81.4 us (0.34)
  waiting for transfers between devices: 152 us -> 0 us
  Pallas kernels: 0 us -> 65.9 us
  other arithmetic: 31 us -> 0.48 us
  matrix products: 30.3 us -> 11.3 us
  between operations: 14.3 us -> 0.78 us
  local copies, waits for them, and re-layouts: 6.82 us -> 2.74 us
  blocking collectives: 3.45 us -> 0 us
    psum x1 -> x0, waiting for transfers between devices: 152 us -> none  [shards(): projections = lax.psum(local_proj, 'tm')]
    pallas_call x0 -> x1, Pallas kernels: none -> 65.9 us  [exchange(): pl.pallas_call(functools.partial(exchange_kernel, modes, tm_bits, sp_bits...]
    another operation x11 -> x1, other arithmetic: 24.2 us -> 0.01 us  [the longest x4 11.1 us: factor_solve(): lax.linalg.triangular_solve(factor, lower_part, left_side=True, lower=Tru...]
    dot_general x8 -> x4, matrix products: 29.5 us -> 11.3 us  [the longest x1 5.78 us: shards(): jnp.dot(basis_b[:, :2 * modes], amp_rows.astype(jnp.bfloat16), preferred_...]
    mul x2 -> x1, other arithmetic: 4 us -> 0.33 us  [shards(): magnitude * jnp.sin(phase_angle)]
    psum x1 -> x0, blocking collectives: 3.45 us -> none  [shards(): self_terms, cross_sums = lax.psum((self_terms, cross_sums), 'space')]
    gather x4 -> x0, local copies, waits for them, and re-layouts: 2.86 us -> none  [the longest x1 0.72 us: fit_terms(): jnp.diagonal(cross[modes:, modes:])]
  transfers between devices with their start and end apart: 1 -> 0, of which waited for: 1 -> 0; matrix products, arithmetic and copies ran while one was open for 8% -> 0% of each run, Pallas kernels for 0% -> 0%
where the time goes in v1:
time: 81.4 us; the launch traced here: 81.2 us
  Pallas kernels  65.9 us (81%)
  matrix products  11.3 us (14%)
  local copies, waits for them, and re-layouts  2.74 us (3%)
    pallas_call x1, Pallas kernels, exchange(): pl.pallas_call(functools.partial(exchange_kernel, modes, tm_bits, sp_bits...  65.9 us
    dot_general x1, matrix products, shards(): jnp.dot(basis_b[:, :2 * modes], amp_rows.astype(jnp.bfloat16), preferred_...  5.78 us
    dot_general x1, matrix products, shards(): lax.dot_general(basis_b, snapshots, (((0,), (0,)), ((), ())), preferred_e...  4.79 us
    unnamed x8, local copies, waits for them, and re-layouts  1.9 us

profile of v1, /device:TPU:0, one launch (start us, length us, event | category | flops | bytes accessed | tf_op | source)
XLA Modules:
  0.0 81.2 jit_solution(2453311834427287490)
XLA Ops:
  0.6 0.0 copy-start
  0.7 0.8 slice_bitcast_fusion.1
  1.4 0.3 fusion.16
  1.8 0.4 fusion.1
  2.2 0.4 fusion.5
  2.6 0.1 pad.4.clone
  2.7 0.1 maximum_maximum_fusion.1.gram_ref
  2.7 0.0 slice-start
  2.8 0.0 slice-start.1
  2.8 4.8 %fusion.8.yz_ref = f32[128,8192]{1,0:T(8,128)S(1)} fusion(bf16[512,8192]{1,0:T(8,128)(2,1)} %param.2, bf16[512,64]{0,1:T(8,128)(2,1)S(1)} %fusion.7, bf16[512,32]{0,1:T(8,128)(2,1)S(1)} %get-tuple-element.11, bf16[512,32]{0,1:T(8,128)(2,1)S(1)} %get-tuple-element.10), kind=kOutput, calls=%fused_computation.11 | convolution fusion | flops 1074135040 | bytes 12713984 | tf_op jit(solution)/shard_map/dot_general | solution.py:328
  7.6 0.0 copy-done
  7.6 65.9 %shard_map.49 = (f32[64,8192]{1,0:T(8,128)S(1)}, f32[2,32]{1,0:T(2,128)S(1)}) custom-call(f32[128,8192]{1,0:T(8,128)S(1)} %fusion.8.yz_ref, f32[64,128]{1,0:T(8,128)S(1)} %maximum_maximum_fusion.1.gram_ref, f32[2,32]{1,0:T(2,128)S(1)} %copy-done), custom_call_target="tpu_custom_call" | custom-call | tf_op jit(solution)/shard_map/pallas_call | solution.py:287
  73.5 0.0 slice-done
  73.5 0.0 slice-done.1
  73.6 5.8 %subtract_convert_fusion = bf16[512,8192]{1,0:T(8,128)(2,1)} fusion(bf16[512,8192]{1,0:T(8,128)(2,1)S(1)} %bitcast.9, f32[64,8192]{1,0:T(8,128)S(1)} %get-tuple-element.6, bf16[512,32]{0,1:T(8,128)(2,1)S(1)} %get-tuple-element.11, bf16[512,32]{0,1:T(8,128)(2,1)S(1)} %get-tuple-element.10), kind=kOutput, calls=%fused_computation | convolution fusion | flops 550109184 | bytes 18939904 | tf_op jit(solution)/shard_map/dot_general | solution.py:340
  79.3 0.6 copy.11
  79.9 1.3 %copy.12 = f32[2,32,8192]{2,1,0:T(8,128)} copy(f32[2,32,8192]{2,1,0:T(8,128)S(1)} %bitcast.7) | data formatting | bytes 4194304
  (8 shorter events, 0.1 us)
Async XLA Ops:
  0.6 6.9 %copy-start = (f32[2,32]{1,0:T(2,128)S(1)}, f32[2,32]{1,0:T(2,128)}, u32[]{:S(2)}) copy-start(f32[2,32]{1,0:T(2,128)} %exps_ref.1) | copy-start | bytes 772
  2.7 70.8 %slice-start = ((s8[8388608]{0:T(1024)(128)(4,1)}), s8[4194304]{0:T(1024)(128)(4,1)S(1)}, s32[]{:S(2)}) async-start(s8[8388608]{0:T(1024)(128)(4,1)} %bitcast.8), calls=%async_computation | async-start | bytes 8388608
  2.8 70.8 %slice-start.1 = ((s8[8388608]{0:T(1024)(128)(4,1)}), s8[4194304]{0:T(1024)(128)(4,1)S(1)}, s32[]{:S(2)}) async-start(s8[8388608]{0:T(1024)(128)(4,1)} %bitcast.8), calls=%async_computation.1 | async-start | bytes 8388608

commit v2 on v1

v2 whole, which is shorter than its diff:
```python
import functools

import jax
import jax.numpy as jnp
from jax import lax
from jax.experimental import pallas as pl
from jax.experimental.pallas import tpu as pltpu
from jax.sharding import PartitionSpec as P

damping = 0.01
MESH = pl.DeviceIdType.MESH
LANES = 128
WAVES = 2
TILE = 512
ORDERS = ((0, 1, 2), (1, 0, 2), (2, 0, 1), (1, 2, 0))


def phases_of(part, tm_bits):
    first = [b for b in ORDERS[part % len(ORDERS)] if b < tm_bits]
    order = first + [b for b in range(tm_bits) if b not in first]
    tail = order[2:]
    return [[b] for b in order[:2]] + [tail[i : i + 2] for i in range(0, len(tail), 2)]


def exact_dot(left, right, dims=((1,), (0,))):
    return lax.dot_general(
        left,
        right,
        (dims, ((), ())),
        precision=lax.Precision.HIGHEST,
        preferred_element_type=jnp.float32,
    )


def complex_inverse(real, imag):
    modes = real.shape[0]
    rows = lax.broadcasted_iota(jnp.int32, real.shape, 0)
    cols = lax.broadcasted_iota(jnp.int32, real.shape, 1)
    for k in range(modes):
        on_row, on_col = rows == k, cols == k
        scale = 1.0 / real[k : k + 1, k : k + 1]
        row_r = jnp.where(on_col[:1], 1.0, real[k : k + 1, :]) * scale
        row_i = jnp.where(on_col[:1], 0.0, imag[k : k + 1, :]) * scale
        col_r, col_i = real[:, k : k + 1], imag[:, k : k + 1]
        real = jnp.where(
            on_row, row_r, jnp.where(on_col, 0.0, real) - (col_r * row_r - col_i * row_i)
        )
        imag = jnp.where(
            on_row, row_i, jnp.where(on_col, 0.0, imag) - (col_r * row_i + col_i * row_r)
        )
    return real, imag


def complex_dot(ar, ai, br, bi):
    return exact_dot(ar, br) - exact_dot(ai, bi), exact_dot(ar, bi) + exact_dot(ai, br)


def exchange_kernel(
    modes, tm_bits, sp_bits, parts,
    x_ref, basis_ref, gram_ref, exps_ref,
    amp_ref, new_ref,
    xbuf, yz_ref, full, halves, gsum, grecv, ssum, srecv, vsum, vnear, vfar,
    rs_send, rs_recv, ag_send, ag_recv,
    g_send, g_recv, s_send, s_recv, n_send, n_recv, f_send, f_recv, x_sem, out_sem,
):
    double = 2 * modes
    columns = full.shape[1]
    width = columns // parts
    band = double // WAVES
    me, sp = lax.axis_index("tm"), lax.axis_index("space")
    swap = sp % 2

    def stride_of(bit):
        if tm_bits >= 2 and bit == 0:
            return 1 + swap
        if tm_bits >= 2 and bit == 1:
            return 2 - swap
        return 2**bit

    def flip(index, stride):
        side = (index // stride) % 2
        return side, index + (1 - 2 * side) * stride

    friends = [(flip(me, 2**b)[1], sp) for b in range(tm_bits)]
    friends += [(me, flip(sp, 2**b)[1]) for b in range(sp_bits)]

    spaces, low = 2**sp_bits, 2 ** (tm_bits // 2)
    n_near, n_far = low * spaces, 2**tm_bits // low
    near_slot, far_slot = (me % low) * spaces + sp, me // low
    near, far = [], []
    for d in range(1, n_near):
        other = (near_slot + d) % n_near
        near.append((far_slot * low + other // spaces, other % spaces))
    for d in range(1, n_far):
        far.append(((far_slot + d) % n_far * low + me % low, sp))

    def lanes(start, size):
        return pl.ds(pl.multiple_of(start, LANES), size)

    plan, mixed = [], set()
    for p in range(parts):
        plan.append([])
        for bits in phases_of(p, tm_bits):
            sides = [flip(me, stride_of(b))[0] for b in bits]
            mine = sum(side * 2**j for j, side in enumerate(sides))
            partners = []
            for mask in range(1, 2 ** len(bits)):
                device, place, chosen = me, mine, []
                for j, b in enumerate(bits):
                    if mask >> j & 1:
                        device = device + (1 - 2 * sides[j]) * stride_of(b)
                        place = place + (1 - 2 * sides[j]) * 2**j
                        chosen.append(b)
                partners.append((device, place))
                mixed.add(tuple(sorted(chosen)))
                mixed.add(tuple(sorted({0: 1, 1: 0}.get(b, b) for b in chosen)))
            plan[p].append((len(bits), mine, partners))
    extra = []
    for chosen in sorted(mixed):
        if min(chosen) < tm_bits // 2 <= max(chosen):
            device = me
            for b in chosen:
                device = device + (1 - 2 * ((me // 2**b) % 2)) * 2**b
            extra.append((device, sp))
    n_phases = len(plan[0])
    sizes = [width]
    for count, _, _ in plan[0]:
        sizes.append(sizes[-1] >> count)

    half = width // 2

    def part_half(p, k):
        side = plan[p][0][1]
        return (1 - side) * half if k == 0 else side * half

    loads = {}
    for k in range(2):
        for p in range(parts):
            at = part_half(p, k)
            loads[p, k] = pltpu.make_async_copy(
                x_ref.at[:, lanes(p * width + at, half)],
                xbuf.at[p, :, lanes(at, half)],
                x_sem.at[p, k],
            )
            loads[p, k].start()

    barrier = pltpu.get_barrier_semaphore()
    for friend in near + far + extra:
        pl.semaphore_signal(barrier, inc=1, device_id=friend, device_id_type=MESH)
    pl.semaphore_wait(barrier, len(near + far + extra))

    def project(p, k):
        loads[p, k].wait()
        at = part_half(p, k)
        tile = min(TILE, half)

        def step(i, carry):
            start = at + i * tile
            yz_ref[:, lanes(p * width + start, tile)] = jnp.dot(
                basis_ref[...],
                xbuf[p, :, lanes(start, tile)],
                preferred_element_type=jnp.float32,
            )
            return carry

        lax.fori_loop(0, half // tile, step, 0)

    def remote(src, dst, send, recv, friend):
        copy = pltpu.make_async_remote_copy(
            src_ref=src, dst_ref=dst, send_sem=send, recv_sem=recv,
            device_id=friend, device_id_type=MESH,
        )
        copy.start()
        return copy

    sends = []

    def sum_start(stage, total, landed, send, recv):
        copy = remote(
            total.at[stage], landed.at[stage], send.at[stage], recv.at[stage], friends[stage]
        )
        sends.append(copy)
        return copy

    def sum_end(stage, copy, total, landed):
        copy.wait_recv()
        total[stage + 1] = total[stage] + landed[stage]

    def scatter_start(p, h, s):
        size = sizes[s + 1]
        rows = pl.ds(h * band, band)
        copies = []
        for m, (device, place) in enumerate(plan[p][s][2]):
            if s == 0:
                src = yz_ref.at[rows, lanes(p * width + place * size, size)]
            else:
                src = halves[s - 1].at[p, 0, rows, lanes(place * size, size)]
            copies.append(
                remote(
                    src, halves[s].at[p, m, rows, :],
                    rs_send.at[p, h, s, m], rs_recv.at[p, h, s, m], (device, sp),
                )
            )
        sends.extend(copies)
        return copies

    def landed(copies):
        for copy in copies:
            copy.wait_recv()

    def scatter_add(p, h, s):
        size = sizes[s + 1]
        _, mine, partners = plan[p][s]
        rows = pl.ds(h * band, band)
        if s == 0:
            total = yz_ref[rows, lanes(p * width + mine * size, size)]
        else:
            total = halves[s - 1][p, 0, rows, lanes(mine * size, size)]
        for m in range(len(partners)):
            total = total + halves[s][p, m, rows, :]
        halves[s][p, 0, rows, :] = total

    gsum[0] = gram_ref[...]
    g_copy = sum_start(0, gsum, grecv, g_send, g_recv)
    flying = {}
    for p in range(parts):
        project(p, 0)
        for h in range(WAVES):
            flying[p, h] = scatter_start(p, h, 0)
    for p in range(parts):
        project(p, 1)
    for s in range(tm_bits):
        sum_end(s, g_copy, gsum, grecv)
        if s + 1 < tm_bits:
            g_copy = sum_start(s + 1, gsum, grecv, g_send, g_recv)
        if s + 1 < n_phases:
            for h in range(WAVES):
                for p in range(parts):
                    landed(flying[p, h])
                    scatter_add(p, h, s)
                    flying[p, h] = scatter_start(p, h, s + 1)

    blocks = gsum[tm_bits]

    def block(index):
        moved = blocks if index == 0 else pltpu.roll(blocks, LANES - index * modes, 1)
        return moved[:modes, :modes], moved[modes:, :modes]

    g_r, g_i = block(0)
    c_r, c_i = block(1)
    e_r, e_i = block(2)
    inv_r, inv_i = complex_inverse(g_r, g_i)
    offsets = []
    last = n_phases - 1

    def gather_start(p, h, s):
        where = full.at[pl.ds(h * band, band), lanes(offsets[p], sizes[s + 1])]
        copies = [
            remote(
                where, where, ag_send.at[p, h, s, m], ag_recv.at[p, h, s, m], (device, sp)
            )
            for m, (device, _) in enumerate(plan[p][s][2])
        ]
        sends.extend(copies)
        return copies

    owned = []
    for p in range(parts):
        for h in range(WAVES):
            landed(flying[p, h])
            scatter_add(p, h, last)
        owned.append(halves[last][p, 0])
        offsets.append(p * width + sum(plan[p][s][1] * sizes[s + 1] for s in range(n_phases)))
    owned = jnp.concatenate(owned, 1)
    own_r, own_i = complex_dot(inv_r, inv_i, owned[:modes], owned[modes:])
    for p in range(parts):
        size = sizes[-1]
        full[pl.ds(0, modes), lanes(offsets[p], size)] = own_r[:, p * size : (p + 1) * size]
        full[pl.ds(modes, modes), lanes(offsets[p], size)] = own_i[:, p * size : (p + 1) * size]
        for h in range(WAVES):
            flying[p, h] = gather_start(p, h, last)
    over = ((1,), (1,))
    self_r = exact_dot(own_r, own_r, over) + exact_dot(own_i, own_i, over)
    self_i = exact_dot(own_r, own_i, over) - exact_dot(own_i, own_r, over)

    ssum[0] = jnp.zeros(ssum.shape[1:], jnp.float32)
    ssum[0, pl.ds(0, modes), pl.ds(0, modes)] = self_r
    ssum[0, pl.ds(modes, modes), pl.ds(0, modes)] = self_i
    s_copy = sum_start(0, ssum, srecv, s_send, s_recv)
    s_stage = 0
    steps = len(friends)
    t_r, t_i = complex_dot(inv_r, inv_i, c_r, c_i)
    u_r, u_i = complex_dot(c_r, c_i, t_r, t_i)
    m_r, m_i = e_r - u_r, e_i - u_i
    for s in range(last, 0, -1):
        for p in range(parts):
            offsets[p] = offsets[p] - plan[p][s][1] * sizes[s + 1]
        for h in range(WAVES):
            for p in range(parts):
                landed(flying[p, h])
                flying[p, h] = gather_start(p, h, s - 1)
        sum_end(s_stage, s_copy, ssum, srecv)
        s_stage += 1
        s_copy = sum_start(s_stage, ssum, srecv, s_send, s_recv)
    while s_stage < steps:
        sum_end(s_stage, s_copy, ssum, srecv)
        s_stage += 1
        if s_stage < steps:
            s_copy = sum_start(s_stage, ssum, srecv, s_send, s_recv)

    s_r = ssum[steps, pl.ds(0, modes), pl.ds(0, modes)]
    s_i = ssum[steps, pl.ds(modes, modes), pl.ds(0, modes)]
    square = (modes, modes)
    diagonal = lax.broadcasted_iota(jnp.int32, square, 0) == lax.broadcasted_iota(
        jnp.int32, square, 1
    )
    h_r = s_r * m_r - s_i * m_i + jnp.where(diagonal, damping, 0.0)
    h_i = s_r * m_i + s_i * m_r
    hinv_r, hinv_i = complex_inverse(h_r, h_i)
    w_r = jnp.sum(c_r * s_r - c_i * s_i, 1, keepdims=True)
    w_i = jnp.sum(c_r * s_i + c_i * s_r, 1, keepdims=True)

    v_r = jnp.zeros((modes, LANES), jnp.float32)
    v_i = jnp.zeros((modes, LANES), jnp.float32)
    outs = []
    for p in range(parts):
        for h in range(WAVES):
            landed(flying[p, h])
        part = pl.ds(p * width, width)
        out = pltpu.make_async_copy(full.at[:, part], amp_ref.at[:, part], out_sem.at[p])
        out.start()
        outs.append(out)
        run = 4

        def step(i, carry, p=p):
            v_r, v_i = carry
            for j in range(run):
                at = lanes(p * width + (i * run + j) * LANES, LANES)
                a_r, a_i = full[pl.ds(0, modes), at], full[pl.ds(modes, modes), at]
                z_r = yz_ref[pl.ds(double, modes), at]
                z_i = yz_ref[pl.ds(double + modes, modes), at]
                v_r = v_r + (a_r * z_r + a_i * z_i)
                v_i = v_i + (a_r * z_i - a_i * z_r)
            return v_r, v_i

        v_r, v_i = lax.fori_loop(0, width // (run * LANES), step, (v_r, v_i))

    ones = jnp.ones((8, LANES), jnp.float32)

    def gather_sum(stage, slots, slot, peers, send, recv):
        copies = []
        for d, peer in enumerate(peers):
            copy = remote(vsum.at[stage], slots.at[slot], send.at[d], recv.at[d], peer)
            copies.append(copy)
            sends.append(copy)
        slots[slot] = vsum[stage]
        for copy in copies:
            copy.wait_recv()
        total = slots[0]
        for k in range(1, len(peers) + 1):
            total = total + slots[k]
        return total

    vsum[0] = jnp.zeros(vsum.shape[1:], jnp.float32)
    vsum[0, :, pl.ds(0, double)] = exact_dot(
        ones, jnp.concatenate([v_r, v_i], 0), ((1,), (1,))
    )
    vsum[1] = gather_sum(0, vnear, near_slot, near, n_send, n_recv)
    v_all = gather_sum(1, vfar, far_slot, far, f_send, f_recv)[:1]

    wide = (modes, LANES)
    spread = lax.broadcasted_iota(jnp.int32, wide, 1) - lax.broadcasted_iota(jnp.int32, wide, 0)

    def as_column(shift):
        return jnp.sum(jnp.where(spread == shift, v_all, 0.0), 1, keepdims=True)

    grad_r = w_r - as_column(0)
    grad_i = w_i - as_column(modes)
    new_ref[pl.ds(0, 1), :] = exps_ref[pl.ds(0, 1), :] - jnp.sum(
        hinv_r * grad_r + hinv_i * grad_i, 0, keepdims=True
    )
    new_ref[pl.ds(1, 1), :] = exps_ref[pl.ds(1, 1), :] - jnp.sum(
        hinv_r * grad_i - hinv_i * grad_r, 0, keepdims=True
    )
    for out in outs:
        out.wait()
    for copy in sends:
        copy.wait_send()


def exchange(snapshots, basis_b, gram, exponents, groups, spaces):
    modes = exponents.shape[1]
    double = 2 * modes
    local_rows, columns = snapshots.shape
    tm_bits, sp_bits = groups.bit_length() - 1, spaces.bit_length() - 1
    assert groups == 2**tm_bits and spaces == 2**sp_bits
    parts = min(len(ORDERS), columns // (groups * LANES))
    steps = tm_bits + sp_bits
    width = columns // parts
    low = 2 ** (tm_bits // 2)
    counts = [len(bits) for bits in phases_of(0, tm_bits)]
    copies = (parts, WAVES, len(counts), 2 ** max(counts) - 1)
    near, far = low * spaces, groups // low

    def buffer(*shape):
        return pltpu.VMEM(shape, jnp.float32)

    def dma(*shape):
        return pltpu.SemaphoreType.DMA(shape)

    vmem = pl.BlockSpec(memory_space=pltpu.VMEM)
    return pl.pallas_call(
        functools.partial(exchange_kernel, modes, tm_bits, sp_bits, parts),
        out_shape=(
            jax.ShapeDtypeStruct((double, columns), jnp.float32),
            jax.ShapeDtypeStruct(exponents.shape, jnp.float32),
        ),
        in_specs=[pl.BlockSpec(memory_space=pl.ANY)] + [vmem] * 3,
        out_specs=(pl.BlockSpec(memory_space=pl.ANY), vmem),
        scratch_shapes=[
            pltpu.VMEM((parts, local_rows, width), snapshots.dtype),
            buffer(2 * double, columns),
            buffer(double, columns),
            [
                buffer(parts, 2**count - 1, double, width >> sum(counts[: s + 1]))
                for s, count in enumerate(counts)
            ],
            buffer(tm_bits + 1, double, LANES),
            buffer(tm_bits, double, LANES),
            buffer(steps + 1, double, LANES),
            buffer(steps, double, LANES),
            buffer(2, 8, LANES),
            buffer(near, 8, LANES),
            buffer(far, 8, LANES),
            dma(*copies), dma(*copies),
            dma(*copies), dma(*copies),
            dma(tm_bits), dma(tm_bits),
            dma(steps), dma(steps),
            dma(near - 1), dma(near - 1),
            dma(far - 1), dma(far - 1),
            dma(parts, 2),
            dma(parts),
        ],
        compiler_params=pltpu.CompilerParams(
            collective_id=0, has_side_effects=True, vmem_limit_bytes=40 * 2**20
        ),
    )(snapshots, basis_b, gram, exponents)


def shards(snapshots, exponents):
    local_rows, columns = snapshots.shape
    modes = exponents.shape[1]
    groups, spaces = lax.axis_size("tm"), lax.axis_size("space")
    rows = lax.axis_index("tm") * local_rows + jnp.arange(local_rows, dtype=jnp.int32)
    time = (rows.astype(jnp.float32) / (local_rows * groups))[None, :]
    magnitude = jnp.exp(time * exponents[0][:, None])
    phase_angle = time * exponents[1][:, None]
    real, imag = magnitude * jnp.cos(phase_angle), magnitude * jnp.sin(phase_angle)
    plain = jnp.concatenate([real, -imag], 0)
    basis_b = jnp.concatenate([plain, time * plain], 0).astype(jnp.bfloat16)
    both = jnp.concatenate([plain, jnp.concatenate([imag, real], 0)], 1)
    twice = jnp.concatenate([time, time], 1)
    first = both[:modes]
    over = ((1,), (1,))
    gram_gc = exact_dot(both, jnp.concatenate([first, twice * first], 0), over)
    gram_e = exact_dot(twice * both, twice * first, over)
    gram = jnp.concatenate(
        [gram_gc, gram_e, jnp.zeros((2 * modes, LANES - 3 * modes), jnp.float32)], 1
    )
    amp_rows, new_exponents = exchange(snapshots, basis_b, gram, exponents, groups, spaces)
    fitted = lax.dot_general(
        basis_b[: 2 * modes],
        amp_rows.astype(jnp.bfloat16),
        (((0,), (0,)), ((), ())),
        preferred_element_type=jnp.float32,
    )
    residual = (snapshots.astype(jnp.float32) - fitted).astype(jnp.bfloat16)
    return (new_exponents, amp_rows.reshape(2, modes, columns), residual)


def solution(mesh):
    return jax.shard_map(
        shards,
        mesh=mesh,
        in_specs=(P("tm", "space"), P()),
        out_specs=(P(), P(None, None, "space"), P("tm", "space")),
        check_vma=False,
    )
```

time: 81.4 us -> 90.7 us (1.11)
  Pallas kernels: 65.9 us -> 76 us
  matrix products: 11.3 us -> 6.5 us
  local copies, waits for them, and re-layouts: 2.74 us -> 6.78 us
    pallas_call x1, Pallas kernels: 65.9 us -> 76 us  [exchange(): pl.pallas_call(functools.partial(exchange_kernel, modes, tm_bits, sp_bits...]
    dot_general x2 -> x1, matrix products: 10.6 us -> 5.78 us  [shards(): lax.dot_general(basis_b[:2 * modes], amp_rows.astype(jnp.bfloat16), (((0,...]
    unnamed x8, local copies, waits for them, and re-layouts: 1.9 us -> 5.94 us
where the time goes in v2:
time: 90.7 us; the launch traced here: 90.5 us
  Pallas kernels  76 us (84%)
  local copies, waits for them, and re-layouts  6.78 us (7%)
  matrix products  6.5 us (7%)
    pallas_call x1, Pallas kernels, exchange(): pl.pallas_call(functools.partial(exchange_kernel, modes, tm_bits, sp_bits...  76 us
    unnamed x8, local copies, waits for them, and re-layouts  5.94 us
    dot_general x1, matrix products, shards(): lax.dot_general(basis_b[:2 * modes], amp_rows.astype(jnp.bfloat16), (((0,...  5.78 us

profile of v2, /device:TPU:0, one launch (start us, length us, event | category | flops | bytes accessed | tf_op | source)
XLA Modules:
  0.0 90.5 jit_solution(15696962666899722921)
XLA Ops:
  0.6 0.8 slice_bitcast_fusion.1
  1.4 0.3 fusion.10
  1.8 0.4 fusion.1
  2.2 0.4 fusion.5
  2.6 0.1 pad.4.clone
  2.6 0.1 maximum_maximum_fusion.1.gram_ref
  2.8 0.0 copy-start
  2.8 3.4 %copy-done = bf16[512,8192]{1,0:T(8,128)(2,1)S(1)} copy-done((bf16[512,8192]{1,0:T(8,128)(2,1)S(1)}, bf16[512,8192]{1,0:T(8,128)(2,1)}, u32[]{:S(2)}) %copy-start) | copy-done | bytes 8388632
  6.1 0.0 copy-start.2
  6.1 0.7 copy-done.2
  6.8 0.0 copy-start.1
  6.8 76.0 %shard_map.49 = (f32[64,8192]{1,0:T(8,128)S(1)}, f32[2,32]{1,0:T(2,128)S(1)}) custom-call(bf16[512,8192]{1,0:T(8,128)(2,1)S(1)} %copy-done, bf16[128,512]{1,0:T(8,128)(2,1)S(1)} %pad_maximum_fusion.basis_ref, f32[64,128]{1,0:T(8,128)S(1)} %maximum_maximum_fusion.1.gram_ref, f32[2,32]{1,0:T(2,128)S(1)} %copy-done.2), custom_call_target="tpu_custom_call" | custom-call | tf_op jit(solution)/shard_map/pallas_call | solution.py:412
  82.8 0.0 copy-done.1
  82.9 5.8 %subtract_convert_fusion = bf16[512,8192]{1,0:T(8,128)(2,1)} fusion(bf16[512,8192]{1,0:T(8,128)(2,1)S(1)} %copy-done.1, f32[64,8192]{1,0:T(8,128)S(1)} %get-tuple-element.6, bf16[32,512]{1,0:T(8,128)(2,1)S(1)} %get-tuple-element.11, bf16[32,512]{1,0:T(8,128)(2,1)S(1)} %get-tuple-element.10), kind=kOutput, calls=%fused_computation | convolution fusion | flops 550109184 | bytes 18939904 | tf_op jit(solution)/shard_map/dot_general | solution.py:471
  88.6 0.6 copy.9
  89.2 1.3 %copy.10 = f32[2,32,8192]{2,1,0:T(8,128)} copy(f32[2,32,8192]{2,1,0:T(8,128)S(1)} %bitcast.6) | data formatting | bytes 4194304
  (8 shorter events, 0.1 us)
Async XLA Ops:
  2.8 3.4 %copy-start = (bf16[512,8192]{1,0:T(8,128)(2,1)S(1)}, bf16[512,8192]{1,0:T(8,128)(2,1)}, u32[]{:S(2)}) copy-start(bf16[512,8192]{1,0:T(8,128)(2,1)} %x_ref.1) | copy-start | bytes 25165828
  6.1 0.7 copy-start.2
  6.8 76.0 %copy-start.1 = (bf16[512,8192]{1,0:T(8,128)(2,1)S(1)}, bf16[512,8192]{1,0:T(8,128)(2,1)}, u32[]{:S(2)}) copy-start(bf16[512,8192]{1,0:T(8,128)(2,1)} %x_ref.1) | copy-start | bytes 25165828
